TPU v7x, 128 devices: a whole 4x4x4 slice. The times are simulated.
128 devices in a mesh: ctx: 32 (over y, x, z_hi), ch: 4 (over z_lo, core).
Axes of the slice: x: 4, y: 4, z: 4 (z_hi: 2, z_lo: 2; z = z_hi * 2 + z_lo), core: 2. Of those that a mesh axis runs over, the one named last changes fastest.
Arguments:
- grad_out: bfloat16 [32, 2, 256, 4096], P('ctx', None, None, 'ch'), may hold values from -6 to 6
- out_weight: bfloat16 [4096, 4096], P('ch'), may hold values from -0.09375 to 0.09375
- gate: bfloat16 [32, 2, 256, 4096], P('ctx', None, None, 'ch'), may hold values from -6 to 6
- filter_taps: float32 [768, 4096], P(None, 'ch'), may hold values from -0.21875 to 0.21875
- doc_starts: int32 [128], replicated, may hold values from 0 to 16384, as said below
Outputs:
- grad_input: float32 [32, 2, 256, 4096], P('ctx', None, None, 'ch')
Inputs may be any that keep to these rules, and one draw needn't show every extreme that they name: `doc_starts`: Non-decreasing; the first is 0; offsets below 16384 start documents, the others equal 16384. Every document is at most 768 tokens long and every one but the last at least 128; one has exactly 768 tokens and one exactly 128.
All inputs are finite; a program needn't handle non-finite values.
Results may differ from a plain program's by a relative error of at most 0.0029.
Values may be sent and summed in bfloat16 or wider, within the bound.
A program may use at most 192 MiB of HBM per device.

v0:
```python
import functools
import math

import jax
import jax.numpy as jnp
import ml_dtypes
import numpy as np
from jax import lax
from jax.experimental import pallas as pl
from jax.experimental.pallas import tpu as pltpu
from jax.sharding import PartitionSpec as P

MESH = pl.DeviceIdType.MESH
BF = jnp.bfloat16
F32 = jnp.float32

CHUNKS = 2
TILE = 256
OWN_L, OWN_U, LX, LZ, LF, UX, UZ, UF = range(8)
S_LX, S_LZ, S_LF, S_UX, S_UZ, S_UF, S_TURN = range(7)


def dft_tables(block):
    order = np.concatenate([np.arange(0, block, 2), np.arange(1, block, 2)])
    omega = 2.0 * math.pi * (order + 0.5) / (2 * block)
    angle = omega[:, None] * np.arange(block)[None, :]
    forward = np.concatenate([np.cos(angle), -np.sin(angle)], axis=0)

    def parts(table):
        high = table.astype(ml_dtypes.bfloat16)
        low = (table - high.astype(np.float64)).astype(ml_dtypes.bfloat16)
        return high, low

    high, low = parts(forward)
    fwd = np.concatenate([high, low, high], axis=1)
    high, low = parts(forward.T / block)
    back = np.concatenate([high, low, high], axis=1)
    return fwd, back


def kernel(
    sizes,
    g_hbm, w_hbm, gate_hbm, taps_hbm, starts_ref, fwd_hbm, back_hbm,
    out_hbm,
    gath, wbuf, gate, taps, fwd, back, pacc, slots, kern, tot, early, masks,
    load_sem, out_sem, ag_send, ag_recv, halo_send, halo_recv,
):
    pairs, block, width, seq = sizes
    n_slots = 4
    rows = 2 * block
    rc = block // CHUNKS
    n_ag = 2 * CHUNKS
    tiles = width // TILE
    last_m = pairs // 2 - 1

    p = lax.axis_index("ctx")
    h = lax.axis_index("ch")
    m = p // 2
    zh = p % 2
    sib_h = h + 1 - 2 * (h % 2)
    zp_h = (h + 2) % 4
    zps_h = (sib_h + 2) % 4
    sib = (p, sib_h)
    zp = (p, zp_h)
    zx = (p + 1 - 2 * zh, h)
    xm = ((p + pairs - 2) % pairs, h)
    xp = ((p + 2) % pairs, h)
    at_turn = m == last_m
    is_last = p == pairs - 1

    loads = [
        pltpu.make_async_copy(fwd_hbm, fwd, load_sem.at[0]),
        pltpu.make_async_copy(taps_hbm, taps, load_sem.at[1]),
        pltpu.make_async_copy(back_hbm, back, load_sem.at[2]),
        pltpu.make_async_copy(gate_hbm, gate, load_sem.at[3]),
        pltpu.make_async_copy(g_hbm, gath.at[:, pl.ds(0, width)], load_sem.at[4]),
    ]
    for i, owner in enumerate((h, sib_h, zp_h, zps_h)):
        loads.append(
            pltpu.make_async_copy(
                w_hbm.at[:, pl.ds(pl.multiple_of(owner * width, width), width)],
                wbuf.at[:, pl.ds(i * width, width)],
                load_sem.at[5 + i],
            )
        )

    barrier = pltpu.get_barrier_semaphore()
    for peer in (sib, zp, zx, xm, xp):
        pl.semaphore_signal(barrier, inc=1, device_id=peer, device_id_type=MESH)
    for cp in loads[:2]:
        cp.start()
    pl.semaphore_wait(barrier, 5)

    def ag_z(k):
        r = pl.ds(k * rc, rc)
        return pltpu.make_async_remote_copy(
            src_ref=g_hbm.at[r],
            dst_ref=gath.at[r, pl.ds(2 * width, width)],
            send_sem=ag_send.at[k],
            recv_sem=ag_recv.at[k],
            device_id=zp,
            device_id_type=MESH,
        )

    def ag_f(k):
        r = pl.ds(k * rc, rc)
        return pltpu.make_async_remote_copy(
            src_ref=gath.at[r, pl.ds(2 * width, width)],
            dst_ref=gath.at[r, pl.ds(3 * width, width)],
            send_sem=ag_send.at[n_ag + k],
            recv_sem=ag_recv.at[n_ag + k],
            device_id=sib,
            device_id_type=MESH,
        )

    ag_s = pltpu.make_async_remote_copy(
        src_ref=g_hbm,
        dst_ref=gath.at[:, pl.ds(width, width)],
        send_sem=ag_send.at[2 * n_ag],
        recv_sem=ag_recv.at[2 * n_ag],
        device_id=sib,
        device_id_type=MESH,
    )
    for k in range(n_ag):
        ag_z(k).start()
    ag_s.start()
    for cp in loads[2:]:
        cp.start()

    def halo(kind, c, src, dst, dev, recv_kind=None):
        r = pl.ds(c * rc, rc)
        return pltpu.make_async_remote_copy(
            src_ref=slots.at[src, r],
            dst_ref=slots.at[dst, r],
            send_sem=halo_send.at[kind, c],
            recv_sem=halo_recv.at[kind if recv_kind is None else recv_kind, c],
            device_id=dev,
            device_id_type=MESH,
        )

    lz_src = jnp.where(zh == 1, OWN_L, LX)
    uz_src = jnp.where(zh == 0, OWN_U, UX)
    lf_src = jnp.where(is_last, OWN_U, LZ)

    def send_lx(c):
        return halo(S_LX, c, OWN_L, LX, xm)

    def send_turn(c):
        return halo(S_TURN, c, OWN_U, LX, zx, S_LX)

    def send_lz(c):
        return halo(S_LZ, c, lz_src, LZ, zx)

    def send_lf(c):
        return halo(S_LF, c, lf_src, LF, xm)

    def send_ux(c):
        return halo(S_UX, c, OWN_U, UX, xp)

    def send_uz(c):
        return halo(S_UZ, c, uz_src, UZ, zx)

    def send_uf(c):
        return halo(S_UF, c, UZ, UF, xp)

    has_lx = jnp.logical_not(is_last)
    does_lx = m > 0
    does_lz = jnp.logical_or(zh == 1, m < last_m)
    has_lz = jnp.logical_or(zh == 0, m < last_m)
    does_lf = m > 0
    has_lf = m < last_m
    does_ux = m < last_m
    has_ux = m > 0
    does_uz = jnp.logical_or(zh == 0, m > 0)
    has_uz = jnp.logical_or(zh == 1, m > 0)
    does_uf = jnp.logical_and(m < last_m, p > 0)
    has_uf = jnp.logical_and(m > 0, p > 2)

    starts = starts_ref[...]

    def doc_rows(base):
        pos = base + lax.broadcasted_iota(jnp.int32, (block, 128), 0)
        return jnp.sum((starts <= pos).astype(F32), axis=1, keepdims=True), pos[:, :1]

    def doc_at(pos):
        return jnp.sum((starts <= pos).astype(F32), axis=1, keepdims=True)

    def put_mask(i, cond):
        masks[i] = jnp.broadcast_to(jnp.where(cond, 1.0, 0.0), (block, TILE)).astype(BF)

    for b in range(2):
        k = p if b == 0 else 2 * pairs - 1 - p
        base = k * block
        first = doc_at(base)
        last = doc_at(base + block - 1)
        own, _ = doc_rows(base)
        put_mask(b * 6 + 0, own == last)
        put_mask(b * 6 + 4, jnp.logical_and(own == first, own != last))
        put_mask(b * 6 + 5, jnp.logical_and(own == first + 1, own != last))
        for d in range(1, 4):
            later, pos = doc_rows(base + d * block)
            put_mask(b * 6 + d, jnp.logical_and(later == last, pos < seq))

    for cp in loads[:2]:
        cp.wait()
    half = block // 2

    def taps_body(t, carry):
        cols = pl.ds(pl.multiple_of(t * TILE, TILE), TILE)
        prev = None
        for b in range(4):
            if b < 3:
                tap = taps[pl.ds(b * block, block), cols]
                high = tap.astype(BF)
                low = (tap - high.astype(F32)).astype(BF)
                spec = jnp.dot(
                    fwd[...],
                    jnp.concatenate([high, high, low], axis=0),
                    preferred_element_type=F32,
                )
                re, im = spec[:block], -spec[block:]
            else:
                re, im = None, None
            if prev is None:
                kre, kim = re, im
            else:
                pre, pim = prev
                turn_re = jnp.concatenate([pim[:half], -pim[half:]], axis=0)
                turn_im = jnp.concatenate([-pre[:half], pre[half:]], axis=0)
                if re is None:
                    kre, kim = turn_re, turn_im
                else:
                    kre, kim = re + turn_re, im + turn_im
            kern[b, pl.ds(0, block), cols] = kre
            kern[b, pl.ds(block, block), cols] = kim
            prev = (re, im)
        return carry

    lax.fori_loop(0, tiles, taps_body, 0)

    loads[4].wait()
    loads[5].wait()
    loads[6].wait()
    ag_s.wait_recv()
    nt = (((1,), (1,)), ((), ()))

    def base_body(t, carry):
        cols = pl.ds(pl.multiple_of(t * TILE, TILE), TILE)
        pacc[:, cols] = lax.dot_general(
            gath[:, pl.ds(0, 2 * width)],
            wbuf[cols, pl.ds(0, 2 * width)],
            nt,
            preferred_element_type=F32,
        )
        return carry

    lax.fori_loop(0, tiles, base_body, 0)

    def project(k):
        b, c = divmod(k, CHUNKS)
        r = pl.ds(k * rc, rc)

        def body(t, carry):
            cols = pl.ds(pl.multiple_of(t * TILE, TILE), TILE)
            part = lax.dot_general(
                gath[r, pl.ds(2 * width, 2 * width)],
                wbuf[cols, pl.ds(2 * width, 2 * width)],
                nt,
                preferred_element_type=F32,
            )
            value = (pacc[r, cols] + part) * gate[r, cols].astype(F32)
            slots[b, pl.ds(c * rc, rc), cols] = value.astype(BF)
            return carry

        lax.fori_loop(0, tiles, body, 0)

    def spectrum(x, mask):
        xm_ = x * mask
        spec = jnp.dot(
            fwd[:, pl.ds(0, 2 * block)],
            jnp.concatenate([xm_, xm_], axis=0),
            preferred_element_type=F32,
        )
        return spec[:block], spec[block:]

    def inverse(tre, tim):
        total = jnp.concatenate([tre, tim], axis=0)
        high = total.astype(BF)
        low = (total - high.astype(F32)).astype(BF)
        return jnp.dot(
            back[...],
            jnp.concatenate([high, high, low], axis=0),
            preferred_element_type=F32,
        )

    def product(d, cols, re, im):
        kre = kern[d, pl.ds(0, block), cols]
        kim = kern[d, pl.ds(block, block), cols]
        return kre * re - kim * im, kre * im + kim * re

    def own_block(b):
        def body(t, carry):
            cols = pl.ds(pl.multiple_of(t * TILE, TILE), TILE)
            x = slots[b, :, cols]
            re, im = spectrum(x, masks[b * 6])
            tre, tim = product(0, cols, re, im)
            tot[b, pl.ds(0, block), cols] = tre
            tot[b, pl.ds(block, block), cols] = tim
            result = None
            for s in (4, 5):
                mask = masks[b * 6 + s]
                re, im = spectrum(x, mask)
                tre, tim = product(0, cols, re, im)
                part = inverse(tre, tim) * mask.astype(F32)
                result = part if result is None else result + part
            early[b, :, cols] = result
            return carry

        lax.fori_loop(0, tiles, body, 0)

    def cross(b, d, slot):
        def body(t, carry):
            cols = pl.ds(pl.multiple_of(t * TILE, TILE), TILE)
            re, im = spectrum(slots[slot, :, cols], masks[b * 6 + d])
            tre, tim = product(d, cols, re, im)
            tot[b, pl.ds(0, block), cols] += tre
            tot[b, pl.ds(block, block), cols] += tim
            return carry

        lax.fori_loop(0, tiles, body, 0)

    def finish(b):
        def body(t, carry):
            cols = pl.ds(pl.multiple_of(t * TILE, TILE), TILE)
            value = inverse(tot[b, pl.ds(0, block), cols], tot[b, pl.ds(block, block), cols])
            early[b, :, cols] += value * masks[b * 6].astype(F32)
            return carry

        lax.fori_loop(0, tiles, body, 0)

    def out_copy(b):
        return pltpu.make_async_copy(early.at[b], out_hbm.at[b], out_sem.at[b])

    def when(cond, fn):
        pl.when(cond)(fn)

    def gather_step(k):
        ag_z(k).wait_recv()
        ag_f(k).start()
        ag_f(k).wait_recv()
        project(k)

    loads[3].wait()
    loads[7].wait()
    loads[8].wait()
    for c in range(CHUNKS):
        gather_step(c)
        when(does_lx, lambda c=c: send_lx(c).start())
    loads[2].wait()
    own_block(0)

    for c in range(CHUNKS):
        gather_step(CHUNKS + c)
        when(does_ux, lambda c=c: send_ux(c).start())

    for c in range(CHUNKS):
        when(has_lx & jnp.logical_not(at_turn), lambda c=c: send_lx(c).wait_recv())
        when(does_lz, lambda c=c: send_lz(c).start())

    @pl.when(is_last)
    def _():
        for c in range(CHUNKS):
            send_turn(c).start()

    for c in range(CHUNKS):
        when(zh == 0, lambda c=c: send_uz(c).start())

    own_block(1)

    for c in range(CHUNKS):
        when(has_ux, lambda c=c: send_ux(c).wait_recv())
        when(jnp.logical_and(zh == 1, m > 0), lambda c=c: send_uz(c).start())

    cross(1, 2, jnp.where(m > 0, UX, OWN_U))
    when(jnp.logical_not(at_turn), lambda: cross(0, 2, LX))

    for c in range(CHUNKS):
        when(has_lz, lambda c=c: send_lz(c).wait_recv())
        when(does_lf, lambda c=c: send_lf(c).start())

    when(jnp.logical_not(at_turn), lambda: cross(0, 1, LZ))

    for c in range(CHUNKS):
        when(has_uz, lambda c=c: send_uz(c).wait_recv())
        when(does_uf, lambda c=c: send_uf(c).start())

    @pl.when(at_turn)
    def _():
        for c in range(CHUNKS):
            when(has_lx, lambda c=c: send_lx(c).wait_recv())
        cross(0, 1, jnp.where(zh == 1, OWN_U, LZ))
        cross(0, 2, jnp.where(zh == 1, UZ, LX))

    for c in range(CHUNKS):
        when(has_lf, lambda c=c: send_lf(c).wait_recv())
    cross(0, 3, jnp.where(at_turn, jnp.where(zh == 1, UX, OWN_U), LF))
    finish(0)
    out_copy(0).start()
    cross(1, 1, jnp.where(p > 0, UZ, OWN_U))
    for c in range(CHUNKS):
        when(has_uf, lambda c=c: send_uf(c).wait_recv())
    cross(1, 3, jnp.where(p > 2, UF, OWN_U))
    finish(1)
    out_copy(1).start()

    for k in range(n_ag):
        ag_z(k).wait_send()
        ag_f(k).wait_send()
    ag_s.wait_send()
    for c in range(CHUNKS):
        when(does_lx, lambda c=c: send_lx(c).wait_send())
        when(does_lz, lambda c=c: send_lz(c).wait_send())
        when(does_lf, lambda c=c: send_lf(c).wait_send())
        when(does_ux, lambda c=c: send_ux(c).wait_send())
        when(does_uz, lambda c=c: send_uz(c).wait_send())
        when(does_uf, lambda c=c: send_uf(c).wait_send())
        when(is_last, lambda c=c: send_turn(c).wait_send())
    out_copy(0).wait()
    out_copy(1).wait()


def on_device(grad_out, out_weight, gate, filter_taps, doc_starts):
    pairs = lax.axis_size("ctx")
    block = grad_out.shape[2]
    width = out_weight.shape[0]
    rows = 2 * block
    features = out_weight.shape[1]
    fwd, back = dft_tables(block)
    any_spec = pl.BlockSpec(memory_space=pl.ANY)
    call = pl.pallas_call(
        functools.partial(kernel, (pairs, block, width, 2 * pairs * block)),
        out_shape=jax.ShapeDtypeStruct((2, block, width), F32),
        in_specs=[
            any_spec, any_spec, any_spec, any_spec,
            pl.BlockSpec(memory_space=pltpu.VMEM),
            any_spec, any_spec,
        ],
        out_specs=any_spec,
        scratch_shapes=[
            pltpu.VMEM((rows, features), BF),
            pltpu.VMEM((width, features), BF),
            pltpu.VMEM((rows, width), BF),
            pltpu.VMEM(filter_taps.shape, F32),
            pltpu.VMEM(fwd.shape, BF),
            pltpu.VMEM(back.shape, BF),
            pltpu.VMEM((rows, width), F32),
            pltpu.VMEM((8, block, width), BF),
            pltpu.VMEM((4, 2 * block, width), F32),
            pltpu.VMEM((2, 2 * block, width), F32),
            pltpu.VMEM((2, block, width), F32),
            pltpu.VMEM((12, block, TILE), BF),
            pltpu.SemaphoreType.DMA((9,)),
            pltpu.SemaphoreType.DMA((2,)),
            pltpu.SemaphoreType.DMA((4 * CHUNKS + 1,)),
            pltpu.SemaphoreType.DMA((4 * CHUNKS + 1,)),
            pltpu.SemaphoreType.DMA((7, CHUNKS)),
            pltpu.SemaphoreType.DMA((6, CHUNKS)),
        ],
        compiler_params=pltpu.CompilerParams(
            collective_id=0, has_side_effects=True, vmem_limit_bytes=56 << 20
        ),
        name="gated_conv_grad",
    )
    result = call(
        grad_out.reshape(rows, width),
        out_weight,
        gate.reshape(rows, width),
        filter_taps,
        doc_starts.reshape(1, -1),
        jnp.asarray(fwd),
        jnp.asarray(back),
    )
    return result[None]


def solution(mesh):
    in_specs = (
        P("ctx", None, None, "ch"),
        P("ch", None),
        P("ctx", None, None, "ch"),
        P(None, "ch"),
        P(),
    )
    out_specs = P("ctx", None, None, "ch")
    return jax.shard_map(
        on_device, mesh=mesh, in_specs=in_specs, out_specs=out_specs, check_vma=False
    )
```

profile of v0, /device:TPU:30, one launch (start us, length us, event | category | flops | bytes accessed | tf_op | source)
XLA Modules:
  0.0 82.8 jit_solution(4333047980212554955)
XLA Ops:
  0.0 79.6 %gated_conv_grad.1 = f32[2,256,1024]{2,1,0:T(8,128)} custom-call(bf16[512,1024]{1,0:T(8,128)(2,1)} %bitcast.5, bf16[1024,4096]{1,0:T(8,128)(2,1)} %w_hbm.1, bf16[512,1024]{1,0:T(8,128)(2,1)} %bitcast.6, f32[768,1024]{1,0:T(8,128)} %taps_hbm.1, s32[1,128]{1,0:T(1,128)} %bitcast.7, bf16[512,768]{1,0:T(8,128)(2,1)} %constant.4.clone.fwd_hbm, ...), custom_call_target="tpu_custom_call" | custom-call | tf_op jit(solution)/shard_map/gated_conv_grad/pallas_call | solution.py:474
  79.7 3.2 %copy.9 = f32[1,2,256,1024]{3,2,1,0:T(8,128)} copy(f32[1,2,256,1024]{3,2,1,0:T(8,128)} %bitcast.4) | data formatting | bytes 4194304
where the time goes:
time: 83.8 us; the launch traced here: 82.8 us
  Pallas kernels  79.6 us (95%)
  local copies, waits for them, and re-layouts  3.16 us (4%)
    pallas_call x1, Pallas kernels, on_device(): call(grad_out.reshape(rows, width), out_weight, gate.reshape(rows, width)...  79.6 us
    unnamed x1, local copies, waits for them, and re-layouts  3.16 us

commit v1 on v0

--- a/solution.py
+++ b/solution.py
@@ -14,10 +14,11 @@
 BF = jnp.bfloat16
 F32 = jnp.float32
 
-CHUNKS = 2
+GATHER = 2
+CHUNKS = 4
 TILE = 256
 OWN_L, OWN_U, LX, LZ, LF, UX, UZ, UF = range(8)
-S_LX, S_LZ, S_LF, S_UX, S_UZ, S_UF, S_TURN = range(7)
+S_LX, S_LZ, S_LF, S_UX, S_UZ, S_UF = range(6)
 
 
 def dft_tables(block):
@@ -40,16 +41,15 @@
 
 def kernel(
     sizes,
-    g_hbm, w_hbm, gate_hbm, taps_hbm, starts_ref, fwd_hbm, back_hbm,
-    out_hbm,
-    gath, wbuf, gate, taps, fwd, back, pacc, slots, kern, tot, early, masks,
-    load_sem, out_sem, ag_send, ag_recv, halo_send, halo_recv,
+    g_hbm, w_hbm, gate_hbm, taps_hbm, starts_hbm, fwd_hbm, back_hbm,
+    out,
+    gath, wbuf, gate, taps, starts_ref, fwd, back, pacc, slots, kern, tot, masks,
+    load_sem, ag_send, ag_recv, halo_send, halo_recv,
 ):
     pairs, block, width, seq = sizes
-    n_slots = 4
-    rows = 2 * block
+    ra = block // GATHER
     rc = block // CHUNKS
-    n_ag = 2 * CHUNKS
+    n_ag = 2 * GATHER
     tiles = width // TILE
     last_m = pairs // 2 - 1
 
@@ -67,6 +67,7 @@
     xp = ((p + 2) % pairs, h)
     at_turn = m == last_m
     is_last = p == pairs - 1
+    turned = p == pairs - 2
 
     loads = [
         pltpu.make_async_copy(fwd_hbm, fwd, load_sem.at[0]),
@@ -83,16 +84,17 @@
                 load_sem.at[5 + i],
             )
         )
+    loads.append(pltpu.make_async_copy(starts_hbm, starts_ref, load_sem.at[9]))
 
     barrier = pltpu.get_barrier_semaphore()
     for peer in (sib, zp, zx, xm, xp):
         pl.semaphore_signal(barrier, inc=1, device_id=peer, device_id_type=MESH)
-    for cp in loads[:2]:
+    for cp in loads[:2] + loads[9:]:
         cp.start()
     pl.semaphore_wait(barrier, 5)
 
     def ag_z(k):
-        r = pl.ds(k * rc, rc)
+        r = pl.ds(k * ra, ra)
         return pltpu.make_async_remote_copy(
             src_ref=g_hbm.at[r],
             dst_ref=gath.at[r, pl.ds(2 * width, width)],
@@ -103,7 +105,7 @@
         )
 
     def ag_f(k):
-        r = pl.ds(k * rc, rc)
+        r = pl.ds(k * ra, ra)
         return pltpu.make_async_remote_copy(
             src_ref=gath.at[r, pl.ds(2 * width, width)],
             dst_ref=gath.at[r, pl.ds(3 * width, width)],
@@ -124,7 +126,7 @@
     for k in range(n_ag):
         ag_z(k).start()
     ag_s.start()
-    for cp in loads[2:]:
+    for cp in loads[2:9]:
         cp.start()
 
     def halo(kind, c, src, dst, dev, recv_kind=None):
@@ -141,12 +143,10 @@
     lz_src = jnp.where(zh == 1, OWN_L, LX)
     uz_src = jnp.where(zh == 0, OWN_U, UX)
     lf_src = jnp.where(is_last, OWN_U, LZ)
+    lx_src = jnp.where(m > 0, OWN_L, UZ)
 
     def send_lx(c):
-        return halo(S_LX, c, OWN_L, LX, xm)
-
-    def send_turn(c):
-        return halo(S_TURN, c, OWN_U, LX, zx, S_LX)
+        return halo(S_LX, c, lx_src, LX, xm)
 
     def send_lz(c):
         return halo(S_LZ, c, lz_src, LZ, zx)
@@ -163,19 +163,18 @@
     def send_uf(c):
         return halo(S_UF, c, UZ, UF, xp)
 
-    has_lx = jnp.logical_not(is_last)
-    does_lx = m > 0
+    does_lx = jnp.logical_or(m > 0, p == 0)
     does_lz = jnp.logical_or(zh == 1, m < last_m)
     has_lz = jnp.logical_or(zh == 0, m < last_m)
     does_lf = m > 0
     has_lf = m < last_m
-    does_ux = m < last_m
-    has_ux = m > 0
-    does_uz = jnp.logical_or(zh == 0, m > 0)
-    has_uz = jnp.logical_or(zh == 1, m > 0)
+    relays = p == 0
+    does_ux = jnp.logical_or(m < last_m, is_last)
+    has_ux = p > 0
     does_uf = jnp.logical_and(m < last_m, p > 0)
     has_uf = jnp.logical_and(m > 0, p > 2)
 
+    loads[9].wait()
     starts = starts_ref[...]
 
     def doc_rows(base):
@@ -257,8 +256,8 @@
     lax.fori_loop(0, tiles, base_body, 0)
 
     def project(k):
-        b, c = divmod(k, CHUNKS)
-        r = pl.ds(k * rc, rc)
+        b, c = divmod(k, GATHER)
+        r = pl.ds(k * ra, ra)
 
         def body(t, carry):
             cols = pl.ds(pl.multiple_of(t * TILE, TILE), TILE)
@@ -269,17 +268,22 @@
                 preferred_element_type=F32,
             )
             value = (pacc[r, cols] + part) * gate[r, cols].astype(F32)
-            slots[b, pl.ds(c * rc, rc), cols] = value.astype(BF)
+            slots[b, pl.ds(c * ra, ra), cols] = value.astype(BF)
             return carry
 
         lax.fori_loop(0, tiles, body, 0)
 
-    def spectrum(x, mask):
+    def spectrum(x, mask, first=0):
+        n = x.shape[0]
         xm_ = x * mask
+        if n == block:
+            table = fwd[:, pl.ds(0, 2 * block)]
+        else:
+            table = jnp.concatenate(
+                [fwd[:, pl.ds(first, n)], fwd[:, pl.ds(block + first, n)]], axis=1
+            )
         spec = jnp.dot(
-            fwd[:, pl.ds(0, 2 * block)],
-            jnp.concatenate([xm_, xm_], axis=0),
-            preferred_element_type=F32,
+            table, jnp.concatenate([xm_, xm_], axis=0), preferred_element_type=F32
         )
         return spec[:block], spec[block:]
 
@@ -298,48 +302,37 @@
         kim = kern[d, pl.ds(block, block), cols]
         return kre * re - kim * im, kre * im + kim * re
 
-    def own_block(b):
-        def body(t, carry):
-            cols = pl.ds(pl.multiple_of(t * TILE, TILE), TILE)
-            x = slots[b, :, cols]
-            re, im = spectrum(x, masks[b * 6])
+    def own_tile(b, t):
+        cols = pl.ds(t * TILE, TILE)
+        x = slots[b, :, cols]
+        re, im = spectrum(x, masks[b * 6])
+        tre, tim = product(0, cols, re, im)
+        tot[b, pl.ds(0, block), cols] = tre
+        tot[b, pl.ds(block, block), cols] = tim
+        result = None
+        for s in (4, 5):
+            mask = masks[b * 6 + s]
+            re, im = spectrum(x, mask)
             tre, tim = product(0, cols, re, im)
-            tot[b, pl.ds(0, block), cols] = tre
-            tot[b, pl.ds(block, block), cols] = tim
-            result = None
-            for s in (4, 5):
-                mask = masks[b * 6 + s]
-                re, im = spectrum(x, mask)
-                tre, tim = product(0, cols, re, im)
-                part = inverse(tre, tim) * mask.astype(F32)
-                result = part if result is None else result + part
-            early[b, :, cols] = result
-            return carry
-
-        lax.fori_loop(0, tiles, body, 0)
-
-    def cross(b, d, slot):
-        def body(t, carry):
-            cols = pl.ds(pl.multiple_of(t * TILE, TILE), TILE)
-            re, im = spectrum(slots[slot, :, cols], masks[b * 6 + d])
+            part = inverse(tre, tim) * mask.astype(F32)
+            result = part if result is None else result + part
+        out[b, :, cols] = result
+
+    def cross(b, d, slot, first=0, count=None):
+        n = block if count is None else count
+        r = pl.ds(first, n)
+        for t in range(tiles):
+            cols = pl.ds(t * TILE, TILE)
+            re, im = spectrum(slots[slot, r, cols], masks[b * 6 + d, r], first)
             tre, tim = product(d, cols, re, im)
             tot[b, pl.ds(0, block), cols] += tre
             tot[b, pl.ds(block, block), cols] += tim
-            return carry
-
-        lax.fori_loop(0, tiles, body, 0)
 
     def finish(b):
-        def body(t, carry):
-            cols = pl.ds(pl.multiple_of(t * TILE, TILE), TILE)
+        for t in range(tiles):
+            cols = pl.ds(t * TILE, TILE)
             value = inverse(tot[b, pl.ds(0, block), cols], tot[b, pl.ds(block, block), cols])
-            early[b, :, cols] += value * masks[b * 6].astype(F32)
-            return carry
-
-        lax.fori_loop(0, tiles, body, 0)
-
-    def out_copy(b):
-        return pltpu.make_async_copy(early.at[b], out_hbm.at[b], out_sem.at[b])
+            out[b, :, cols] += value * masks[b * 6].astype(F32)
 
     def when(cond, fn):
         pl.when(cond)(fn)
@@ -350,68 +343,85 @@
         ag_f(k).wait_recv()
         project(k)
 
+    per = CHUNKS // GATHER
+
+    def ux_to_uz(c):
+        when(has_ux, lambda: send_ux(c).wait_recv())
+        when(zh == 1, lambda: send_uz(c).start())
+
+    def lz_to_lf(c):
+        when(has_lz, lambda: send_lz(c).wait_recv())
+        when(does_lf, lambda: send_lf(c).start())
+
+    def uz_to_uf(c):
+        send_uz(c).wait_recv()
+        when(does_uf, lambda: send_uf(c).start())
+        when(relays, lambda: send_lx(c).start())
+
     loads[3].wait()
     loads[7].wait()
     loads[8].wait()
-    for c in range(CHUNKS):
-        gather_step(c)
-        when(does_lx, lambda c=c: send_lx(c).start())
+    for k in range(GATHER):
+        gather_step(k)
+        for c in range(k * per, (k + 1) * per):
+            when(m > 0, lambda c=c: send_lx(c).start())
     loads[2].wait()
-    own_block(0)
-
-    for c in range(CHUNKS):
-        gather_step(CHUNKS + c)
-        when(does_ux, lambda c=c: send_ux(c).start())
-
-    for c in range(CHUNKS):
-        when(has_lx & jnp.logical_not(at_turn), lambda c=c: send_lx(c).wait_recv())
-        when(does_lz, lambda c=c: send_lz(c).start())
-
-    @pl.when(is_last)
-    def _():
-        for c in range(CHUNKS):
-            send_turn(c).start()
-
+    for t in range(tiles):
+        own_tile(0, t)
+
+    for k in range(GATHER):
+        gather_step(GATHER + k)
+        for c in range(k * per, (k + 1) * per):
+            when(does_ux, lambda c=c: send_ux(c).start())
+        if k == GATHER - 2:
+            for c in range(CHUNKS):
+                when(jnp.logical_not(at_turn), lambda c=c: send_lx(c).wait_recv())
+                when(does_lz, lambda c=c: send_lz(c).start())
     for c in range(CHUNKS):
         when(zh == 0, lambda c=c: send_uz(c).start())
 
-    own_block(1)
-
-    for c in range(CHUNKS):
-        when(has_ux, lambda c=c: send_ux(c).wait_recv())
-        when(jnp.logical_and(zh == 1, m > 0), lambda c=c: send_uz(c).start())
-
+    when(jnp.logical_not(at_turn), lambda: cross(0, 2, LX))
+    ux_to_uz(0)
+    ux_to_uz(1)
+    lz_to_lf(0)
+    own_tile(1, 0)
+    lz_to_lf(1)
+    own_tile(1, 1)
+    ux_to_uz(2)
+    lz_to_lf(2)
+    own_tile(1, 2)
+    ux_to_uz(3)
+    lz_to_lf(3)
+    own_tile(1, 3)
+    cross(0, 1, jnp.where(is_last, OWN_U, LZ))
+    uz_to_uf(0)
     cross(1, 2, jnp.where(m > 0, UX, OWN_U))
-    when(jnp.logical_not(at_turn), lambda: cross(0, 2, LX))
-
-    for c in range(CHUNKS):
-        when(has_lz, lambda c=c: send_lz(c).wait_recv())
-        when(does_lf, lambda c=c: send_lf(c).start())
-
-    when(jnp.logical_not(at_turn), lambda: cross(0, 1, LZ))
-
-    for c in range(CHUNKS):
-        when(has_uz, lambda c=c: send_uz(c).wait_recv())
-        when(does_uf, lambda c=c: send_uf(c).start())
-
-    @pl.when(at_turn)
-    def _():
-        for c in range(CHUNKS):
-            when(has_lx, lambda c=c: send_lx(c).wait_recv())
-        cross(0, 1, jnp.where(zh == 1, OWN_U, LZ))
-        cross(0, 2, jnp.where(zh == 1, UZ, LX))
-
+    uz_to_uf(1)
     for c in range(CHUNKS):
         when(has_lf, lambda c=c: send_lf(c).wait_recv())
     cross(0, 3, jnp.where(at_turn, jnp.where(zh == 1, UX, OWN_U), LF))
-    finish(0)
-    out_copy(0).start()
+    uz_to_uf(2)
+    when(jnp.logical_not(at_turn), lambda: finish(0))
+    uz_to_uf(3)
     cross(1, 1, jnp.where(p > 0, UZ, OWN_U))
-    for c in range(CHUNKS):
-        when(has_uf, lambda c=c: send_uf(c).wait_recv())
-    cross(1, 3, jnp.where(p > 2, UF, OWN_U))
+
+    @pl.when(is_last)
+    def _():
+        cross(0, 2, UZ)
+        finish(0)
+
+    for j in range(2):
+        for c in range(2 * j, 2 * j + 2):
+            when(has_uf, lambda c=c: send_uf(c).wait_recv())
+        cross(1, 3, jnp.where(p > 2, UF, OWN_U), j * (block // 2), block // 2)
     finish(1)
-    out_copy(1).start()
+
+    @pl.when(turned)
+    def _():
+        for c in range(CHUNKS):
+            send_lx(c).wait_recv()
+        cross(0, 2, LX)
+        finish(0)
 
     for k in range(n_ag):
         ag_z(k).wait_send()
@@ -422,11 +432,8 @@
         when(does_lz, lambda c=c: send_lz(c).wait_send())
         when(does_lf, lambda c=c: send_lf(c).wait_send())
         when(does_ux, lambda c=c: send_ux(c).wait_send())
-        when(does_uz, lambda c=c: send_uz(c).wait_send())
+        send_uz(c).wait_send()
         when(does_uf, lambda c=c: send_uf(c).wait_send())
-        when(is_last, lambda c=c: send_turn(c).wait_send())
-    out_copy(0).wait()
-    out_copy(1).wait()
 
 
 def on_device(grad_out, out_weight, gate, filter_taps, doc_starts):
@@ -436,42 +443,37 @@
     rows = 2 * block
     features = out_weight.shape[1]
     fwd, back = dft_tables(block)
-    any_spec = pl.BlockSpec(memory_space=pl.ANY)
+    hbm = pl.BlockSpec(memory_space=pltpu.HBM)
     call = pl.pallas_call(
         functools.partial(kernel, (pairs, block, width, 2 * pairs * block)),
         out_shape=jax.ShapeDtypeStruct((2, block, width), F32),
-        in_specs=[
-            any_spec, any_spec, any_spec, any_spec,
-            pl.BlockSpec(memory_space=pltpu.VMEM),
-            any_spec, any_spec,
-        ],
-        out_specs=any_spec,
+        in_specs=[hbm] * 7,
+        out_specs=pl.BlockSpec(memory_space=pltpu.VMEM),
         scratch_shapes=[
             pltpu.VMEM((rows, features), BF),
             pltpu.VMEM((width, features), BF),
             pltpu.VMEM((rows, width), BF),
             pltpu.VMEM(filter_taps.shape, F32),
+            pltpu.VMEM((1, doc_starts.shape[0]), jnp.int32),
             pltpu.VMEM(fwd.shape, BF),
             pltpu.VMEM(back.shape, BF),
             pltpu.VMEM((rows, width), F32),
             pltpu.VMEM((8, block, width), BF),
             pltpu.VMEM((4, 2 * block, width), F32),
             pltpu.VMEM((2, 2 * block, width), F32),
-            pltpu.VMEM((2, block, width), F32),
             pltpu.VMEM((12, block, TILE), BF),
-            pltpu.SemaphoreType.DMA((9,)),
-            pltpu.SemaphoreType.DMA((2,)),
-            pltpu.SemaphoreType.DMA((4 * CHUNKS + 1,)),
-            pltpu.SemaphoreType.DMA((4 * CHUNKS + 1,)),
-            pltpu.SemaphoreType.DMA((7, CHUNKS)),
+            pltpu.SemaphoreType.DMA((10,)),
+            pltpu.SemaphoreType.DMA((4 * GATHER + 1,)),
+            pltpu.SemaphoreType.DMA((4 * GATHER + 1,)),
+            pltpu.SemaphoreType.DMA((6, CHUNKS)),
             pltpu.SemaphoreType.DMA((6, CHUNKS)),
         ],
         compiler_params=pltpu.CompilerParams(
-            collective_id=0, has_side_effects=True, vmem_limit_bytes=56 << 20
+            collective_id=0, has_side_effects=True, vmem_limit_bytes=44 << 20
         ),
         name="gated_conv_grad",
     )
-    result = call(
+    operands = (
         grad_out.reshape(rows, width),
         out_weight,
         gate.reshape(rows, width),
@@ -480,6 +482,7 @@
         jnp.asarray(fwd),
         jnp.asarray(back),
     )
+    result = call(*[pltpu.with_memory_space_constraint(v, pltpu.HBM) for v in operands])
     return result[None]
 
 

time: 83.8 us -> 64.5 us (0.77); the launches traced: 82.8 us -> 64.4 us
  Pallas kernels: 79.6 us -> 63.1 us
  local copies, waits for them, and re-layouts: 3.16 us -> 1.32 us
    pallas_call x1, Pallas kernels: 79.6 us -> 63.1 us  [on_device(): call(*[pltpu.with_memory_space_constraint(v, pltpu.HBM) for v in operands])]
    unnamed x1, local copies, waits for them, and re-layouts: 3.16 us -> 1.32 us
where the time goes in v1:
time: 64.5 us; the launch traced here: 64.4 us
  Pallas kernels  63.1 us (98%)
  local copies, waits for them, and re-layouts  1.32 us (2%)
    pallas_call x1, Pallas kernels, on_device(): call(*[pltpu.with_memory_space_constraint(v, pltpu.HBM) for v in operands])  63.1 us
    unnamed x1, local copies, waits for them, and re-layouts  1.32 us

profile of v1, /device:TPU:30, one launch (start us, length us, event | category | flops | bytes accessed | tf_op | source)
XLA Modules:
  0.0 64.4 jit_solution(8684842977441336894)
XLA Ops:
  0.0 63.1 %gated_conv_grad.1 = f32[2,256,1024]{2,1,0:T(8,128)S(1)} custom-call(bf16[512,1024]{1,0:T(8,128)(2,1)} %bitcast.5, bf16[1024,4096]{1,0:T(8,128)(2,1)} %w_hbm.1, bf16[512,1024]{1,0:T(8,128)(2,1)} %bitcast.6, f32[768,1024]{1,0:T(8,128)} %taps_hbm.1, s32[1,128]{1,0:T(1,128)} %bitcast.7, bf16[512,768]{1,0:T(8,128)(2,1)} %constant.4.clone.fwd_hbm, ...), custom_call_target="tpu_custom_call" | custom-call | tf_op jit(solution)/shard_map/gated_conv_grad/pallas_call | solution.py:485
  63.1 1.3 %copy.9 = f32[1,2,256,1024]{3,2,1,0:T(8,128)} copy(f32[1,2,256,1024]{3,2,1,0:T(8,128)S(1)} %bitcast.4) | data formatting | bytes 4194304

commit v2 on v1

--- a/solution.py
+++ b/solution.py
@@ -15,7 +15,8 @@
 F32 = jnp.float32
 
 GATHER = 2
-CHUNKS = 4
+PIECES = ((0, 64), (64, 64), (128, 64), (192, 32), (224, 32))
+CHUNKS = len(PIECES)
 TILE = 256
 OWN_L, OWN_U, LX, LZ, LF, UX, UZ, UF = range(8)
 S_LX, S_LZ, S_LF, S_UX, S_UZ, S_UF = range(6)
@@ -48,7 +49,6 @@
 ):
     pairs, block, width, seq = sizes
     ra = block // GATHER
-    rc = block // CHUNKS
     n_ag = 2 * GATHER
     tiles = width // TILE
     last_m = pairs // 2 - 1
@@ -130,7 +130,7 @@
         cp.start()
 
     def halo(kind, c, src, dst, dev, recv_kind=None):
-        r = pl.ds(c * rc, rc)
+        r = pl.ds(*PIECES[c])
         return pltpu.make_async_remote_copy(
             src_ref=slots.at[src, r],
             dst_ref=slots.at[dst, r],
@@ -253,7 +253,7 @@
         )
         return carry
 
-    lax.fori_loop(0, tiles, base_body, 0)
+    lax.fori_loop(0, tiles, base_body, 0, unroll=True)
 
     def project(k):
         b, c = divmod(k, GATHER)
@@ -271,7 +271,7 @@
             slots[b, pl.ds(c * ra, ra), cols] = value.astype(BF)
             return carry
 
-        lax.fori_loop(0, tiles, body, 0)
+        lax.fori_loop(0, tiles, body, 0, unroll=True)
 
     def spectrum(x, mask, first=0):
         n = x.shape[0]
@@ -334,6 +334,21 @@
             value = inverse(tot[b, pl.ds(0, block), cols], tot[b, pl.ds(block, block), cols])
             out[b, :, cols] += value * masks[b * 6].astype(F32)
 
+    def late(b, d, slot, first=0, count=None):
+        n = block if count is None else count
+        r = pl.ds(first, n)
+        for t in range(tiles):
+            cols = pl.ds(t * TILE, TILE)
+            re, im = spectrum(slots[slot, r, cols], masks[b * 6 + d, r], first)
+            tre, tim = product(d, cols, re, im)
+            high = jnp.concatenate([tre, tim], axis=0).astype(BF)
+            value = jnp.dot(
+                back[:, pl.ds(0, 4 * block)],
+                jnp.concatenate([high, high], axis=0),
+                preferred_element_type=F32,
+            )
+            out[b, :, cols] += value * masks[b * 6].astype(F32)
+
     def when(cond, fn):
         pl.when(cond)(fn)
 
@@ -343,14 +358,15 @@
         ag_f(k).wait_recv()
         project(k)
 
-    per = CHUNKS // GATHER
+    def pieces_of(k):
+        return [c for c, (first, _) in enumerate(PIECES) if first // ra == k]
 
     def ux_to_uz(c):
         when(has_ux, lambda: send_ux(c).wait_recv())
         when(zh == 1, lambda: send_uz(c).start())
 
     def lz_to_lf(c):
-        when(has_lz, lambda: send_lz(c).wait_recv())
+        when(has_lz & (p > 0), lambda: send_lz(c).wait_recv())
         when(does_lf, lambda: send_lf(c).start())
 
     def uz_to_uf(c):
@@ -363,7 +379,7 @@
     loads[8].wait()
     for k in range(GATHER):
         gather_step(k)
-        for c in range(k * per, (k + 1) * per):
+        for c in pieces_of(k):
             when(m > 0, lambda c=c: send_lx(c).start())
     loads[2].wait()
     for t in range(tiles):
@@ -371,12 +387,13 @@
 
     for k in range(GATHER):
         gather_step(GATHER + k)
-        for c in range(k * per, (k + 1) * per):
+        for c in pieces_of(k):
             when(does_ux, lambda c=c: send_ux(c).start())
         if k == GATHER - 2:
             for c in range(CHUNKS):
                 when(jnp.logical_not(at_turn), lambda c=c: send_lx(c).wait_recv())
-                when(does_lz, lambda c=c: send_lz(c).start())
+                first = does_lz if c < 3 else does_lz & (p != 1)
+                when(first, lambda c=c: send_lz(c).start())
     for c in range(CHUNKS):
         when(zh == 0, lambda c=c: send_uz(c).start())
 
@@ -391,37 +408,46 @@
     lz_to_lf(2)
     own_tile(1, 2)
     ux_to_uz(3)
+    ux_to_uz(4)
+    for c in range(3, CHUNKS):
+        when(p == 1, lambda c=c: send_lz(c).start())
     lz_to_lf(3)
+    lz_to_lf(4)
     own_tile(1, 3)
-    cross(0, 1, jnp.where(is_last, OWN_U, LZ))
+    when(p > 0, lambda: cross(0, 1, jnp.where(is_last, OWN_U, LZ)))
     uz_to_uf(0)
     cross(1, 2, jnp.where(m > 0, UX, OWN_U))
     uz_to_uf(1)
     for c in range(CHUNKS):
         when(has_lf, lambda c=c: send_lf(c).wait_recv())
     cross(0, 3, jnp.where(at_turn, jnp.where(zh == 1, UX, OWN_U), LF))
+    half_rows = block // 2
+    uz_slot = jnp.where(p > 0, UZ, OWN_U)
+    uf_slot = jnp.where(p > 2, UF, OWN_U)
+    cross(1, 1, uz_slot, 0, half_rows)
     uz_to_uf(2)
-    when(jnp.logical_not(at_turn), lambda: finish(0))
+    finish(0)
     uz_to_uf(3)
-    cross(1, 1, jnp.where(p > 0, UZ, OWN_U))
-
-    @pl.when(is_last)
-    def _():
-        cross(0, 2, UZ)
-        finish(0)
-
-    for j in range(2):
-        for c in range(2 * j, 2 * j + 2):
-            when(has_uf, lambda c=c: send_uf(c).wait_recv())
-        cross(1, 3, jnp.where(p > 2, UF, OWN_U), j * (block // 2), block // 2)
+    uz_to_uf(4)
+    cross(1, 1, uz_slot, half_rows, half_rows)
+    for c in range(2):
+        when(has_uf, lambda c=c: send_uf(c).wait_recv())
+    cross(1, 3, uf_slot, 0, half_rows)
     finish(1)
-
-    @pl.when(turned)
+    for c in range(2, CHUNKS):
+        when(has_uf, lambda c=c: send_uf(c).wait_recv())
+    late(1, 3, uf_slot, half_rows, half_rows)
+
+    @pl.when(at_turn | relays)
     def _():
         for c in range(CHUNKS):
-            send_lx(c).wait_recv()
-        cross(0, 2, LX)
-        finish(0)
+            when(turned, lambda c=c: send_lx(c).wait_recv())
+            when(relays, lambda c=c: send_lz(c).wait_recv())
+        late(
+            0,
+            jnp.where(relays, 1, 2),
+            jnp.where(relays, LZ, jnp.where(zh == 1, UZ, LX)),
+        )
 
     for k in range(n_ag):
         ag_z(k).wait_send()

time: 64.5 us -> 62.5 us (0.969); the launches traced: 64.4 us -> 61.6 us
  Pallas kernels: 63.1 us -> 60.3 us
    pallas_call x1, Pallas kernels: 63.1 us -> 60.3 us  [on_device(): call(*[pltpu.with_memory_space_constraint(v, pltpu.HBM) for v in operands])]
where the time goes in v2:
time: 62.5 us; the launch traced here: 61.6 us
  Pallas kernels  60.3 us (96%)
  local copies, waits for them, and re-layouts  1.32 us (2%)
    pallas_call x1, Pallas kernels, on_device(): call(*[pltpu.with_memory_space_constraint(v, pltpu.HBM) for v in operands])  60.3 us
    unnamed x1, local copies, waits for them, and re-layouts  1.32 us

profile of v2, /device:TPU:30, one launch (start us, length us, event | category | flops | bytes accessed | tf_op | source)
XLA Modules:
  0.0 61.6 jit_solution(4377894142885241007)
XLA Ops:
  0.0 60.3 %gated_conv_grad.1 = f32[2,256,1024]{2,1,0:T(8,128)S(1)} custom-call(bf16[512,1024]{1,0:T(8,128)(2,1)} %bitcast.5, bf16[1024,4096]{1,0:T(8,128)(2,1)} %w_hbm.1, bf16[512,1024]{1,0:T(8,128)(2,1)} %bitcast.6, f32[768,1024]{1,0:T(8,128)} %taps_hbm.1, s32[1,128]{1,0:T(1,128)} %bitcast.7, bf16[512,768]{1,0:T(8,128)(2,1)} %constant.4.clone.fwd_hbm, ...), custom_call_target="tpu_custom_call" | custom-call | tf_op jit(solution)/shard_map/gated_conv_grad/pallas_call | solution.py:511
  60.3 1.3 %copy.9 = f32[1,2,256,1024]{3,2,1,0:T(8,128)} copy(f32[1,2,256,1024]{3,2,1,0:T(8,128)S(1)} %bitcast.4) | data formatting | bytes 4194304

commit v3 on v2

--- a/solution.py
+++ b/solution.py
@@ -288,12 +288,10 @@
         return spec[:block], spec[block:]
 
     def inverse(tre, tim):
-        total = jnp.concatenate([tre, tim], axis=0)
-        high = total.astype(BF)
-        low = (total - high.astype(F32)).astype(BF)
+        high = jnp.concatenate([tre, tim], axis=0).astype(BF)
         return jnp.dot(
-            back[...],
-            jnp.concatenate([high, high, low], axis=0),
+            back[:, pl.ds(0, 4 * block)],
+            jnp.concatenate([high, high], axis=0),
             preferred_element_type=F32,
         )
 

time: 62.5 us -> 61.7 us (0.987)
  no operation moved by 1% of the time
where the time goes in v3:
time: 61.7 us; the launch traced here: 61.2 us
  Pallas kernels  59.8 us (97%)
  local copies, waits for them, and re-layouts  1.32 us (2%)
    pallas_call x1, Pallas kernels, on_device(): call(*[pltpu.with_memory_space_constraint(v, pltpu.HBM) for v in operands])  59.8 us
    unnamed x1, local copies, waits for them, and re-layouts  1.32 us

profile of v3, /device:TPU:30, one launch (start us, length us, event | category | flops | bytes accessed | tf_op | source)
XLA Modules:
  0.0 61.2 jit_solution(1459545675252809764)
XLA Ops:
  0.0 59.8 %gated_conv_grad.1 = f32[2,256,1024]{2,1,0:T(8,128)S(1)} custom-call(bf16[512,1024]{1,0:T(8,128)(2,1)} %bitcast.5, bf16[1024,4096]{1,0:T(8,128)(2,1)} %w_hbm.1, bf16[512,1024]{1,0:T(8,128)(2,1)} %bitcast.6, f32[768,1024]{1,0:T(8,128)} %taps_hbm.1, s32[1,128]{1,0:T(1,128)} %bitcast.7, bf16[512,768]{1,0:T(8,128)(2,1)} %constant.4.clone.fwd_hbm, ...), custom_call_target="tpu_custom_call" | custom-call | tf_op jit(solution)/shard_map/gated_conv_grad/pallas_call | solution.py:509
  59.8 1.3 %copy.9 = f32[1,2,256,1024]{3,2,1,0:T(8,128)} copy(f32[1,2,256,1024]{3,2,1,0:T(8,128)S(1)} %bitcast.4) | data formatting | bytes 4194304

commit v4 on v3

--- a/solution.py
+++ b/solution.py
@@ -255,6 +255,17 @@
 
     lax.fori_loop(0, tiles, base_body, 0, unroll=True)
 
+    def near_part(k):
+        r = pl.ds(k * ra, ra)
+        for t in range(tiles):
+            cols = pl.ds(t * TILE, TILE)
+            pacc[r, cols] += lax.dot_general(
+                gath[r, pl.ds(2 * width, width)],
+                wbuf[cols, pl.ds(2 * width, width)],
+                nt,
+                preferred_element_type=F32,
+            )
+
     def project(k):
         b, c = divmod(k, GATHER)
         r = pl.ds(k * ra, ra)
@@ -262,8 +273,8 @@
         def body(t, carry):
             cols = pl.ds(pl.multiple_of(t * TILE, TILE), TILE)
             part = lax.dot_general(
-                gath[r, pl.ds(2 * width, 2 * width)],
-                wbuf[cols, pl.ds(2 * width, 2 * width)],
+                gath[r, pl.ds(3 * width, width)],
+                wbuf[cols, pl.ds(3 * width, width)],
                 nt,
                 preferred_element_type=F32,
             )
@@ -341,8 +352,8 @@
             tre, tim = product(d, cols, re, im)
             high = jnp.concatenate([tre, tim], axis=0).astype(BF)
             value = jnp.dot(
-                back[:, pl.ds(0, 4 * block)],
-                jnp.concatenate([high, high], axis=0),
+                back[:, pl.ds(0, 2 * block)],
+                high,
                 preferred_element_type=F32,
             )
             out[b, :, cols] += value * masks[b * 6].astype(F32)
@@ -353,6 +364,7 @@
     def gather_step(k):
         ag_z(k).wait_recv()
         ag_f(k).start()
+        near_part(k)
         ag_f(k).wait_recv()
         project(k)
 

time: 61.7 us -> 61.3 us (level)
  no operation moved by 1% of the time
where the time goes in v4:
time: 61.3 us; the launch traced here: 61.2 us
  Pallas kernels  59.9 us (98%)
  local copies, waits for them, and re-layouts  1.32 us (2%)
    pallas_call x1, Pallas kernels, on_device(): call(*[pltpu.with_memory_space_constraint(v, pltpu.HBM) for v in operands])  59.9 us
    unnamed x1, local copies, waits for them, and re-layouts  1.32 us

profile of v4, /device:TPU:30, one launch (start us, length us, event | category | flops | bytes accessed | tf_op | source)
XLA Modules:
  0.0 61.2 jit_solution(5990401309963116576)
XLA Ops:
  0.0 59.9 %gated_conv_grad.1 = f32[2,256,1024]{2,1,0:T(8,128)S(1)} custom-call(bf16[512,1024]{1,0:T(8,128)(2,1)} %bitcast.5, bf16[1024,4096]{1,0:T(8,128)(2,1)} %w_hbm.1, bf16[512,1024]{1,0:T(8,128)(2,1)} %bitcast.6, f32[768,1024]{1,0:T(8,128)} %taps_hbm.1, s32[1,128]{1,0:T(1,128)} %bitcast.7, bf16[512,768]{1,0:T(8,128)(2,1)} %constant.4.clone.fwd_hbm, ...), custom_call_target="tpu_custom_call" | custom-call | tf_op jit(solution)/shard_map/gated_conv_grad/pallas_call | solution.py:521
  59.9 1.3 %copy.9 = f32[1,2,256,1024]{3,2,1,0:T(8,128)} copy(f32[1,2,256,1024]{3,2,1,0:T(8,128)S(1)} %bitcast.4) | data formatting | bytes 4194304
